TPU v7x, 32 devices: a whole 2x2x4 slice. The times are simulated.
32 devices in a mesh: mp: 2 (over x), width: 2 (over y), hidden: 8 (over z, core).
Axes of the slice: x: 2, y: 2, z: 4, core: 2. Of those that a mesh axis runs over, the one named last changes fastest.
Arguments:
- residual_in: bfloat16 [2, 512, 3584], P('mp', 'hidden'), may hold values from -6 to 6
- gate_weight: bfloat16 [2, 14336, 3584], P('mp', ('width', 'hidden')), may hold values from -0.09375 to 0.09375
- up_weight: bfloat16 [2, 14336, 3584], P('mp', ('width', 'hidden')), may hold values from -0.09375 to 0.09375
- down_weight: bfloat16 [2, 14336, 3584], P('mp', ('width', 'hidden')), may hold values from -0.046875 to 0.046875
- enc_weight: float32 [7168, 16384], P(('mp', 'width'), 'hidden'), may hold values from -0.0625 to 0.0625
- enc_bias: float32 [16384], P('hidden'), may hold values from -3 to 3
- dec_weight: float32 [16384, 7168], P('hidden', ('mp', 'width')), may hold values from -0.25 to 0.25
- dec_bias: float32 [7168], P(('mp', 'width')), may hold values from -2 to 2
Outputs:
- mlp_acts: bfloat16 [2, 512, 3584], P('mp', 'hidden', 'width')
- latents: float32 [512, 16384], P(None, 'hidden')
- grad_enc: float32 [7168, 16384], P(('mp', 'width'), 'hidden')
- grad_dec: float32 [16384, 7168], P('hidden', ('mp', 'width'))
- grad_enc_bias: float32 [16384], P('hidden')
- grad_dec_bias: float32 [7168], P(('mp', 'width'))
All inputs are finite; a program needn't handle non-finite values.
Results may differ from a plain program's by a relative error of at most 0.0058.
Values may be sent and summed in bfloat16 or wider, within the bound.
A program may use at most 192 MiB of HBM per device.

v0:
```python
import jax
import jax.numpy as jnp
from jax import lax
from jax.sharding import PartitionSpec as P

TOKENS = 512
sharpness = 8.0
sparsity_coef = 0.02
norm_floor = 1e-06
highest = lax.Precision.HIGHEST


def body(
    residual_in, gate_weight, up_weight, down_weight, enc_weight, enc_bias, dec_weight, dec_bias
):
    last_last = (((1,), (1,)), ((), ()))
    first_first = (((0,), (0,)), ((), ()))
    gathered = lax.all_gather(residual_in[0], "hidden", axis=0, tiled=True)
    gate_act = lax.dot_general(
        gathered, gate_weight[0], last_last, preferred_element_type=jnp.float32
    )
    up_act = lax.dot_general(gathered, up_weight[0], last_last, preferred_element_type=jnp.float32)
    hidden_act = (jax.nn.gelu(gate_act, approximate=True) * up_act).astype(jnp.bfloat16)
    down_local = down_weight[0]
    row_sums = lax.psum_scatter(
        jnp.dot(hidden_act, down_local, preferred_element_type=jnp.float32),
        "hidden",
        scatter_dimension=0,
        tiled=True,
    )
    model_sums = lax.psum_scatter(row_sums, "width", scatter_dimension=1, tiled=True)
    mlp_acts = model_sums.astype(jnp.bfloat16)
    coder_in = lax.all_gather(mlp_acts, "hidden", axis=0, tiled=True).astype(jnp.float32)
    enc_partial = jnp.dot(coder_in, enc_weight, precision=highest)
    model_index = lax.axis_index("mp")
    squares = jnp.sum(dec_weight * dec_weight, axis=1)
    square_pair = jnp.where(jnp.arange(2)[:, None] == model_index, squares[None, :], 0.0)
    pre_sum, square_sums = lax.psum((enc_partial, square_pair), ("mp", "width"))
    pre_act = pre_sum + enc_bias
    latents = jax.nn.softplus(sharpness * pre_act) / sharpness
    dec_norms = jnp.sqrt(square_sums + norm_floor)
    recon_part = jnp.dot(latents, dec_weight, precision=highest)
    own_rebuilt = lax.psum_scatter(recon_part, "hidden", scatter_dimension=0, tiled=True) + dec_bias
    own_grad = 2.0 / TOKENS * (own_rebuilt - mlp_acts.astype(jnp.float32))
    err_grad = lax.all_gather(own_grad.astype(jnp.bfloat16), "hidden", axis=0, tiled=True).astype(
        own_grad.dtype
    )
    grad_dec_bias = jnp.sum(err_grad, axis=0)
    back_part = lax.dot_general(
        err_grad, dec_weight, last_last, precision=highest, preferred_element_type=jnp.float32
    )
    lat_grad = lax.psum(back_part.astype(jnp.bfloat16), ("mp", "width")).astype(
        jnp.float32
    ) + sparsity_coef * (dec_norms[0] + dec_norms[1])
    pre_grad = lat_grad * jax.nn.sigmoid(sharpness * pre_act)
    grad_enc_bias = jnp.sum(pre_grad, axis=0)
    grad_enc = lax.dot_general(
        coder_in, pre_grad, first_first, precision=highest, preferred_element_type=jnp.float32
    )
    latent_totals = jnp.sum(latents, axis=0)
    own_norm = jnp.where(model_index == 0, dec_norms[0], dec_norms[1])
    grad_dec = lax.dot_general(
        latents, err_grad, first_first, precision=highest, preferred_element_type=jnp.float32
    )
    grad_dec = grad_dec + sparsity_coef * (latent_totals / own_norm)[:, None] * dec_weight
    return (mlp_acts[None], latents, grad_enc, grad_dec, grad_enc_bias, grad_dec_bias)


def solution(mesh):
    return jax.shard_map(
        body,
        mesh=mesh,
        in_specs=(
            P("mp", "hidden", None),
            P("mp", ("width", "hidden"), None),
            P("mp", ("width", "hidden"), None),
            P("mp", ("width", "hidden"), None),
            P(("mp", "width"), "hidden"),
            P("hidden"),
            P("hidden", ("mp", "width")),
            P(("mp", "width")),
        ),
        out_specs=(
            P("mp", "hidden", "width"),
            P(None, "hidden"),
            P(("mp", "width"), "hidden"),
            P("hidden", ("mp", "width")),
            P("hidden"),
            P(("mp", "width")),
        ),
        check_vma=False,
    )
```

profile of v0, /device:TPU:0, one launch (start us, length us, event | category | flops | bytes accessed | tf_op | source)
XLA Modules:
  0.0 549.1 jit_solution(14673929088239518730)
XLA Ops:
  7.2 0.0 all-gather.9.cloned.1.call-start
  7.2 0.7 all-gather.9.cloned.1.call-update
  7.9 0.0 reduce-scatter.4.cloned.1.call-start
  7.9 47.0 %all-gather.9.cloned.1.call-done = bf16[1,512,3584]{2,1,0:T(8,128)(2,1)} async-done(((bf16[1,64,3584]{2,1,0:T(8,128)(2,1)}), bf16[1,512,3584]{2,1,0:T(8,128)(2,1)}) %all-gather.9.cloned.1.call-update) | async-done | bytes 3670032 | tf_op jit(solution)/shard_map/all_gather | solution.py:18
  54.9 0.0 copy-start.7
  54.9 0.0 slice-start
  54.9 9.6 %fusion.4 = f32[512,896]{1,0:T(8,128)S(1)} fusion(bf16[1,896,3584]{2,1,0:T(8,128)(2,1)} %param.9, bf16[1,512,3584]{2,1,0:T(8,128)(2,1)} %all-gather.9.cloned.1.call-done), kind=kOutput, calls=%fused_computation.7 | convolution fusion | flops 3288334336 | bytes 11927552 | tf_op jit(solution)/shard_map/dot_general | solution.py:19
  64.5 0.0 copy-done.7
  64.6 0.0 slice-start.1
  64.6 7.1 %fusion.17 = bf16[512,896]{1,0:T(8,128)(2,1)S(1)} fusion(f32[512,896]{1,0:T(8,128)S(1)} %fusion.4, bf16[1,896,3584]{2,1,0:T(8,128)(2,1)} %param.10, bf16[1,512,3584]{2,1,0:T(8,128)(2,1)S(1)} %copy-done.7), kind=kOutput, calls=%fused_computation.25 | convolution fusion | flops 3292921856 | bytes 12845056 | tf_op jit(solution)/shard_map/dot_general | solution.py:22
  71.7 0.0 slice-done
  71.7 0.0 slice-done.1
  71.7 6.0 %fusion = f32[512,3584]{1,0:T(8,128)} fusion(bf16[512,896]{1,0:T(8,128)(2,1)S(1)} %fusion.17, bf16[1,896,3584]{2,1,0:T(8,128)(2,1)S(1)} %bitcast.36), kind=kOutput, calls=%fused_computation.3 | convolution fusion | flops 3288334336 | bytes 14680064 | tf_op jit(solution)/shard_map/dot_general | solution.py:26
  77.8 0.0 reduce-scatter.4.cloned.1.call-update
  77.8 0.0 reduce-scatter.6.cloned.1.call-start
  77.9 78.6 %reduce-scatter.4.cloned.1.call-done = f32[64,3584]{1,0:T(8,128)} async-done(((f32[512,3584]{1,0:T(8,128)}), f32[64,3584]{1,0:T(8,128)}) %reduce-scatter.4.cloned.1.call-update) | async-done | bytes 917520 | tf_op jit(solution)/shard_map/reduce_scatter | solution.py:25
  156.4 0.0 reduce-scatter.6.cloned.1.call-update
  156.4 0.0 all-gather.5.cloned.1.call-start
  156.5 19.6 %reduce-scatter.6.cloned.1.call-done = f32[64,1792]{1,0:T(8,128)} async-done(((f32[64,3584]{1,0:T(8,128)}), f32[64,1792]{1,0:T(8,128)}) %reduce-scatter.6.cloned.1.call-update) | async-done | bytes 458768 | tf_op jit(solution)/shard_map/reduce_scatter | solution.py:31
  176.1 1.7 convert_element_type.23
  177.8 0.0 all-gather.5.cloned.1.call-update
  177.9 0.3 all-reduce.3.cloned.1.call-start
  178.2 27.0 %all-gather.5.cloned.1.call-done = bf16[512,1792]{1,0:T(8,128)(2,1)} async-done(((bf16[64,1792]{1,0:T(8,128)(2,1)}), bf16[512,1792]{1,0:T(8,128)(2,1)}) %all-gather.5.cloned.1.call-update) | async-done | bytes 1835024 | tf_op jit(solution)/shard_map/all_gather | solution.py:33
  205.2 16.9 %fusion.26 = f32[512,2048]{1,0:T(8,128)} fusion(bf16[512,1792]{1,0:T(8,128)(2,1)} %all-gather.5.cloned.1.call-done, f32[1792,2048]{1,0:T(8,128)} %param.12), kind=kOutput, calls=%fused_computation.36 | convolution fusion | flops 22548578304 | bytes 20709376 | tf_op jit(solution)/shard_map/dot_general | solution.py:34
  222.1 0.0 copy-start.5
  222.1 0.0 all-reduce.3.cloned.1.call-update
  222.1 0.4 reduce-scatter.8.cloned.1.call-start
  222.5 102.8 %all-reduce.3.cloned.1.call-done = f32[512,2048]{1,0:T(8,128)} async-done(((f32[512,2048]{1,0:T(8,128)}), f32[512,2048]{1,0:T(8,128)}) %all-reduce.3.cloned.1.call-update) | async-done | bytes 4194320 | tf_op jit(solution)/shard_map/psum | solution.py:38
  325.3 0.0 copy-done.5
  325.3 4.9 fusion.24
  330.2 0.0 copy-start
  330.2 2.0 copy-done
  332.2 0.0 copy-start.3
  332.2 0.0 copy-start.6
  332.2 26.6 %fusion.27 = f32[512,1792]{1,0:T(8,128)} fusion(f32[512,2048]{1,0:T(8,128)S(1)} %get-tuple-element.7, f32[2048,1792]{1,0:T(8,128)} %param.14), kind=kOutput, calls=%fused_computation.37 | convolution fusion | flops 22548578304 | bytes 22544384 | tf_op jit(solution)/shard_map/dot_general | solution.py:42
  358.9 0.0 reduce-scatter.8.cloned.1.call-update
  358.9 0.0 all-gather.7.cloned.1.call-start
  359.0 45.1 %reduce-scatter.8.cloned.1.call-done = f32[64,1792]{1,0:T(8,128)} async-done(((f32[512,1792]{1,0:T(8,128)}), f32[64,1792]{1,0:T(8,128)}) %reduce-scatter.8.cloned.1.call-update) | async-done | bytes 458768 | tf_op jit(solution)/shard_map/reduce_scatter | solution.py:43
  404.0 0.0 copy-done.3
  404.0 0.0 copy-done.6
  404.1 1.8 multiply_convert_fusion
  405.8 0.0 all-gather.7.cloned.1.call-update
  405.8 0.0 all-reduce.5.cloned.1.call-start
  405.9 6.2 %multiply_reduce_fusion = f32[2048]{0:T(1024)S(1)} fusion(f32[2048,1792]{1,0:T(8,128)} %param.14), kind=kLoop, calls=%fused_computation.1 | loop fusion | flops 7337984 | bytes 14688256 | tf_op jit(solution)/shard_map/reduce_sum | solution.py:36
  412.1 0.1 broadcast_select_fusion
  412.2 16.5 %psum.23 = f32[2,2048]{1,0:T(2,128)S(1)} all-reduce(f32[2,2048]{1,0:T(2,128)S(1)} %broadcast_select_fusion), channel_id=1, replica_groups=mesh['mp'=2,'width'=2,'hidden'=8] {'mp','width'}, use_global_device_ids=true, to_apply=%region_6.7 | all-reduce | flops 4096 | bytes 32768 | tf_op jit(solution)/shard_map/psum | solution.py:38
  428.8 2.9 all-gather.7.cloned.1.call-done
  431.7 0.0 copy-start.2
  431.7 18.4 %convolution_convert_fusion = bf16[512,2048]{1,0:T(8,128)(2,1)} fusion(bf16[512,1792]{1,0:T(8,128)(2,1)} %all-gather.7.cloned.1.call-done, f32[2048,1792]{1,0:T(8,128)} %param.14), kind=kOutput, calls=%fused_computation.15 | convolution fusion | flops 22549626880 | bytes 18612224 | tf_op jit(solution)/shard_map/dot_general | solution.py:49
  450.1 0.0 all-reduce.5.cloned.1.call-update
  450.1 0.7 convert_bitcast_fusion
  450.8 0.0 copy-done.2
  450.8 0.9 convert_reduce_fusion
  451.7 19.6 %multiply_add_fusion = f32[2048,1792]{1,0:T(8,128)} fusion(f32[2048,1792]{1,0:T(8,128)} %param.14, f32[512,2048]{1,0:T(8,128)} %copy-done, bf16[512,1792]{1,0:T(8,128)(2,1)S(1)} %copy-done.2, f32[2048]{0:T(1024)S(1)} %divide_multiply_fusion.1), kind=kOutput, calls=%fused_computation | convolution fusion | flops 22555918336 | bytes 35397632 | tf_op jit(solution)/shard_map/dot_general | solution.py:62
  471.3 47.8 %all-reduce.5.cloned.1.call-done = bf16[512,2048]{1,0:T(8,128)(2,1)} async-done(((bf16[512,2048]{1,0:T(8,128)(2,1)}), bf16[512,2048]{1,0:T(8,128)(2,1)}) %all-reduce.5.cloned.1.call-update) | async-done | bytes 2097168 | tf_op jit(solution)/shard_map/psum | solution.py:52
  519.1 0.0 copy-start.1
  519.1 0.0 copy-start.4
  519.2 5.0 fusion.22
  524.1 0.0 copy-done.1
  524.1 0.0 copy-done.4
  524.1 17.9 %fusion.23 = f32[1792,2048]{1,0:T(8,128)} fusion(bf16[512,1792]{1,0:T(8,128)(2,1)} %all-gather.5.cloned.1.call-done, bf16[512,2048]{1,0:T(8,128)(2,1)S(1)} %copy-done.4, f32[512,2048]{1,0:T(8,128)S(1)} %copy-done.1, f32[2048]{0:T(1024)S(1)} %bitcast.33, f32[2048]{0:T(1024)S(1)} %copy-done.5), kind=kOutput, calls=%fused_computation.34 | convolution fusion | flops 22556966912 | bytes 22822912 | tf_op jit(solution)/shard_map/dot_general | solution.py:57
  (5 shorter events, 0.1 us)
Async XLA Ops:
  7.2 47.7 %all-gather.9.cloned.1.call-start = ((), (), s32[]{:S(2)}) async-start(), calls=%async_computation.10 | async-start | bytes 4128768 | tf_op jit(solution)/shard_map/all_gather | solution.py:18
  7.9 148.5 %reduce-scatter.4.cloned.1.call-start = ((), (), s32[]{:S(2)}) async-start(), calls=%async_computation.3 | async-start | bytes 8257536 | tf_op jit(solution)/shard_map/reduce_scatter | solution.py:25
  54.9 9.6 %copy-start.7 = (bf16[1,512,3584]{2,1,0:T(8,128)(2,1)S(1)}, bf16[1,512,3584]{2,1,0:T(8,128)(2,1)}, u32[]{:S(2)}) copy-start(bf16[1,512,3584]{2,1,0:T(8,128)(2,1)} %all-gather.9.cloned.1.call-done) | copy-start | bytes 11010052
  54.9 16.8 %slice-start = ((s8[6422528]{0:T(1024)(128)(4,1)}), s8[4194304]{0:T(1024)(128)(4,1)S(1)}, s32[]{:S(2)}) async-start(s8[6422528]{0:T(1024)(128)(4,1)} %bitcast.35), calls=%async_computation.11 | async-start | bytes 8388608
  64.6 7.2 %slice-start.1 = ((s8[6422528]{0:T(1024)(128)(4,1)}), s8[2228224]{0:T(1024)(128)(4,1)S(1)}, s32[]{:S(2)}) async-start(s8[6422528]{0:T(1024)(128)(4,1)} %bitcast.35), calls=%async_computation.12 | async-start | bytes 4456448
  77.8 98.3 %reduce-scatter.6.cloned.1.call-start = ((), (), s32[]{:S(2)}) async-start(), calls=%async_computation.4 | async-start | bytes 1376256 | tf_op jit(solution)/shard_map/reduce_scatter | solution.py:31
  156.4 48.8 %all-gather.5.cloned.1.call-start = ((), (), s32[]{:S(2)}) async-start(), calls=%async_computation.5 | async-start | bytes 2064384 | tf_op jit(solution)/shard_map/all_gather | solution.py:33
  177.9 147.4 %all-reduce.3.cloned.1.call-start = ((), (), s32[]{:S(2)}) async-start(), calls=%async_computation.6 | async-start | bytes 8388608 | tf_op jit(solution)/shard_map/psum | solution.py:38
  222.1 103.2 %copy-start.5 = (f32[2048]{0:T(1024)S(1)}, f32[2048]{0:T(1024)}, u32[]{:S(2)}) copy-start(f32[2048]{0:T(1024)} %param.13) | copy-start | bytes 24580
  222.1 181.9 %reduce-scatter.8.cloned.1.call-start = ((), (), s32[]{:S(2)}) async-start(), calls=%async_computation.7 | async-start | bytes 4128768 | tf_op jit(solution)/shard_map/reduce_scatter | solution.py:43
  330.2 2.0 copy-start
  332.2 71.8 %copy-start.3 = (f32[64,1792]{1,0:T(8,128)S(1)}, f32[64,1792]{1,0:T(8,128)}, u32[]{:S(2)}) copy-start(f32[64,1792]{1,0:T(8,128)} %reduce-scatter.6.cloned.1.call-done) | copy-start | bytes 1376260
  332.2 71.8 %copy-start.6 = (f32[1792]{0:T(1024)S(1)}, f32[1792]{0:T(1024)}, u32[]{:S(2)}) copy-start(f32[1792]{0:T(1024)} %param.15) | copy-start | bytes 21508
  358.9 72.7 %all-gather.7.cloned.1.call-start = ((), (), s32[]{:S(2)}) async-start(), calls=%async_computation.8 | async-start | bytes 2064384 | tf_op jit(solution)/shard_map/all_gather | solution.py:45
  405.8 113.3 %all-reduce.5.cloned.1.call-start = ((), (), s32[]{:S(2)}) async-start(), calls=%async_computation.9 | async-start | bytes 4194304 | tf_op jit(solution)/shard_map/psum | solution.py:52
  431.7 19.2 %copy-start.2 = (bf16[512,1792]{1,0:T(8,128)(2,1)S(1)}, bf16[512,1792]{1,0:T(8,128)(2,1)}, u32[]{:S(2)}) copy-start(bf16[512,1792]{1,0:T(8,128)(2,1)} %all-gather.7.cloned.1.call-done) | copy-start | bytes 5505028
  519.1 5.0 copy-start.1
  519.1 5.0 copy-start.4
Sparse Core Ops, SparseCore 0:
  9.6 45.2 all-gather.8
  77.9 78.4 reduce-scatter.3
  158.7 17.3 reduce-scatter.5
  178.2 26.9 all-gather.4
  222.2 103.0 all-reduce.2
  359.0 44.9 reduce-scatter.7
  406.3 25.3 all-gather.6
  450.2 68.8 all-reduce.4
where the time goes:
time: 555 us; the launch traced here: 549 us
  waiting for transfers between devices  372 us (67%)
  matrix products  122 us (22%)
  other arithmetic  21.3 us (4%)
  blocking collectives  16.5 us (3%)
  between operations  14.5 us (3%)
    psum x1, waiting for transfers between devices, body(): pre_sum, square_sums = lax.psum((enc_partial, square_pair), ('mp', 'width'))  103 us
    reduce_scatter x1, waiting for transfers between devices, body(): lax.psum_scatter(jnp.dot(hidden_act, down_local, preferred_element_type=j...  78.6 us
    psum x1, waiting for transfers between devices, body(): lax.psum(back_part.astype(jnp.bfloat16), ('mp', 'width'))  47.8 us
    all_gather x1, waiting for transfers between devices, body(): gathered = lax.all_gather(residual_in[0], 'hidden', axis=0, tiled=True)  47 us
    reduce_scatter x1, waiting for transfers between devices, body(): lax.psum_scatter(recon_part, 'hidden', scatter_dimension=0, tiled=True)  45.1 us
    all_gather x1, waiting for transfers between devices, body(): lax.all_gather(mlp_acts, 'hidden', axis=0, tiled=True).astype(jnp.float32)  27 us
    dot_general x1, matrix products, body(): recon_part = jnp.dot(latents, dec_weight, precision=highest)  26.6 us
    reduce_scatter x1, waiting for transfers between devices, body(): lax.psum_scatter(row_sums, 'width', scatter_dimension=1, tiled=True)  19.6 us
  transfers between devices with their start and end apart: 8, of which 8 were waited for; matrix products, arithmetic and copies ran while one was open for 5% of the time, Pallas kernels for 0%

commit v1 on v0

--- a/solution.py
+++ b/solution.py
@@ -1,3 +1,4 @@
+import functools
 import jax
 import jax.numpy as jnp
 from jax import lax
@@ -8,6 +9,14 @@
 sparsity_coef = 0.02
 norm_floor = 1e-06
 highest = lax.Precision.HIGHEST
+
+
+def define_the_pipes(matrix, bus_axis, ax_name):
+    latest = jax.lax.psum(matrix, bus_axis)
+    return jax.lax.psum(latest, ax_name)
+
+
+_write_stocks = functools.partial(define_the_pipes, bus_axis="width", ax_name="mp")
 
 
 def body(
@@ -49,9 +58,9 @@
     back_part = lax.dot_general(
         err_grad, dec_weight, last_last, precision=highest, preferred_element_type=jnp.float32
     )
-    lat_grad = lax.psum(back_part.astype(jnp.bfloat16), ("mp", "width")).astype(
-        jnp.float32
-    ) + sparsity_coef * (dec_norms[0] + dec_norms[1])
+    lat_grad = _write_stocks(back_part.astype(jnp.bfloat16)).astype(jnp.float32) + sparsity_coef * (
+        dec_norms[0] + dec_norms[1]
+    )
     pre_grad = lat_grad * jax.nn.sigmoid(sharpness * pre_act)
     grad_enc_bias = jnp.sum(pre_grad, axis=0)
     grad_enc = lax.dot_general(

time: 555 us -> 612 us (1.10)
  waiting for transfers between devices: 372 us -> 431 us
    psum x1 -> x2, waiting for transfers between devices: 47.8 us -> 84.7 us  [the longest x1 44.8 us: define_the_pipes(): return jax.lax.psum(latest, ax_name)]
    all_gather x1, waiting for transfers between devices: 2.86 us -> 25.2 us  [body(): lax.all_gather(own_grad.astype(jnp.bfloat16), 'hidden', axis=0, tiled=True)]
  transfers between devices with their start and end apart: 8 -> 9, of which waited for: 8 -> 9; matrix products, arithmetic and copies ran while one was open for 5% -> 4% of each run, Pallas kernels for 0% -> 0%
where the time goes in v1:
time: 612 us; the launch traced here: 606 us
  waiting for transfers between devices  431 us (70%)
  matrix products  120 us (20%)
  other arithmetic  21.6 us (4%)
  blocking collectives  16.4 us (3%)
  between operations  14.2 us (2%)
    psum x1, waiting for transfers between devices, body(): pre_sum, square_sums = lax.psum((enc_partial, square_pair), ('mp', 'width'))  103 us
    reduce_scatter x1, waiting for transfers between devices, body(): lax.psum_scatter(jnp.dot(hidden_act, down_local, preferred_element_type=j...  78.6 us
    all_gather x1, waiting for transfers between devices, body(): gathered = lax.all_gather(residual_in[0], 'hidden', axis=0, tiled=True)  47 us
    reduce_scatter x1, waiting for transfers between devices, body(): lax.psum_scatter(recon_part, 'hidden', scatter_dimension=0, tiled=True)  45.1 us
    psum x1, waiting for transfers between devices, define_the_pipes(): return jax.lax.psum(latest, ax_name)  44.8 us
    psum x1, waiting for transfers between devices, define_the_pipes(): latest = jax.lax.psum(matrix, bus_axis)  40 us
    all_gather x1, waiting for transfers between devices, body(): lax.all_gather(mlp_acts, 'hidden', axis=0, tiled=True).astype(jnp.float32)  27 us
    dot_general x1, matrix products, body(): recon_part = jnp.dot(latents, dec_weight, precision=highest)  26.6 us
  transfers between devices with their start and end apart: 9, of which 9 were waited for; matrix products, arithmetic and copies ran while one was open for 4% of the time, Pallas kernels for 0%

profile of v1, /device:TPU:0, one launch (start us, length us, event | category | flops | bytes accessed | tf_op | source)
XLA Modules:
  0.0 606.2 jit_solution(2779686343507140764)
XLA Ops:
  7.2 0.0 all-gather.9.cloned.1.call-start
  7.2 0.7 all-gather.9.cloned.1.call-update
  7.9 0.0 reduce-scatter.4.cloned.1.call-start
  7.9 47.0 %all-gather.9.cloned.1.call-done = bf16[1,512,3584]{2,1,0:T(8,128)(2,1)} async-done(((bf16[1,64,3584]{2,1,0:T(8,128)(2,1)}), bf16[1,512,3584]{2,1,0:T(8,128)(2,1)}) %all-gather.9.cloned.1.call-update) | async-done | bytes 3670032 | tf_op jit(solution)/shard_map/all_gather | solution.py:27
  54.9 0.0 copy-start.7
  54.9 0.0 slice-start
  54.9 9.6 %fusion.4 = f32[512,896]{1,0:T(8,128)S(1)} fusion(bf16[1,896,3584]{2,1,0:T(8,128)(2,1)} %param.9, bf16[1,512,3584]{2,1,0:T(8,128)(2,1)} %all-gather.9.cloned.1.call-done), kind=kOutput, calls=%fused_computation.7 | convolution fusion | flops 3288334336 | bytes 11927552 | tf_op jit(solution)/shard_map/dot_general | solution.py:28
  64.5 0.0 copy-done.7
  64.6 0.0 slice-start.1
  64.6 7.1 %fusion.17 = bf16[512,896]{1,0:T(8,128)(2,1)S(1)} fusion(f32[512,896]{1,0:T(8,128)S(1)} %fusion.4, bf16[1,896,3584]{2,1,0:T(8,128)(2,1)} %param.10, bf16[1,512,3584]{2,1,0:T(8,128)(2,1)S(1)} %copy-done.7), kind=kOutput, calls=%fused_computation.25 | convolution fusion | flops 3292921856 | bytes 12845056 | tf_op jit(solution)/shard_map/dot_general | solution.py:31
  71.7 0.0 slice-done
  71.7 0.0 slice-done.1
  71.7 6.0 fusion
  77.8 0.0 reduce-scatter.4.cloned.1.call-update
  77.8 0.0 reduce-scatter.6.cloned.1.call-start
  77.9 78.6 %reduce-scatter.4.cloned.1.call-done = f32[64,3584]{1,0:T(8,128)} async-done(((f32[512,3584]{1,0:T(8,128)}), f32[64,3584]{1,0:T(8,128)}) %reduce-scatter.4.cloned.1.call-update) | async-done | bytes 917520 | tf_op jit(solution)/shard_map/reduce_scatter | solution.py:34
  156.4 0.0 reduce-scatter.6.cloned.1.call-update
  156.4 0.0 all-gather.5.cloned.1.call-start
  156.5 19.6 %reduce-scatter.6.cloned.1.call-done = f32[64,1792]{1,0:T(8,128)} async-done(((f32[64,3584]{1,0:T(8,128)}), f32[64,1792]{1,0:T(8,128)}) %reduce-scatter.6.cloned.1.call-update) | async-done | bytes 458768 | tf_op jit(solution)/shard_map/reduce_scatter | solution.py:40
  176.1 1.7 convert_element_type.23
  177.8 0.0 all-gather.5.cloned.1.call-update
  177.9 0.3 all-reduce.4.cloned.1.call-start
  178.2 27.0 %all-gather.5.cloned.1.call-done = bf16[512,1792]{1,0:T(8,128)(2,1)} async-done(((bf16[64,1792]{1,0:T(8,128)(2,1)}), bf16[512,1792]{1,0:T(8,128)(2,1)}) %all-gather.5.cloned.1.call-update) | async-done | bytes 1835024 | tf_op jit(solution)/shard_map/all_gather | solution.py:42
  205.2 16.9 %fusion.26 = f32[512,2048]{1,0:T(8,128)} fusion(bf16[512,1792]{1,0:T(8,128)(2,1)} %all-gather.5.cloned.1.call-done, f32[1792,2048]{1,0:T(8,128)} %param.12), kind=kOutput, calls=%fused_computation.36 | convolution fusion | flops 22548578304 | bytes 20709376 | tf_op jit(solution)/shard_map/dot_general | solution.py:43
  222.1 0.0 copy-start.5
  222.1 0.0 all-reduce.4.cloned.1.call-update
  222.1 0.4 reduce-scatter.8.cloned.1.call-start
  222.5 102.8 %all-reduce.4.cloned.1.call-done = f32[512,2048]{1,0:T(8,128)} async-done(((f32[512,2048]{1,0:T(8,128)}), f32[512,2048]{1,0:T(8,128)}) %all-reduce.4.cloned.1.call-update) | async-done | bytes 4194320 | tf_op jit(solution)/shard_map/psum | solution.py:47
  325.3 0.0 copy-done.5
  325.3 4.9 fusion.24
  330.2 0.0 copy-start
  330.2 2.0 copy-done
  332.2 0.0 copy-start.3
  332.2 0.0 copy-start.6
  332.2 26.6 %fusion.27 = f32[512,1792]{1,0:T(8,128)} fusion(f32[512,2048]{1,0:T(8,128)S(1)} %get-tuple-element.7, f32[2048,1792]{1,0:T(8,128)} %param.14), kind=kOutput, calls=%fused_computation.37 | convolution fusion | flops 22548578304 | bytes 22544384 | tf_op jit(solution)/shard_map/dot_general | solution.py:51
  358.9 0.0 reduce-scatter.8.cloned.1.call-update
  358.9 0.0 all-gather.7.cloned.1.call-start
  358.9 45.1 %reduce-scatter.8.cloned.1.call-done = f32[64,1792]{1,0:T(8,128)} async-done(((f32[512,1792]{1,0:T(8,128)}), f32[64,1792]{1,0:T(8,128)}) %reduce-scatter.8.cloned.1.call-update) | async-done | bytes 458768 | tf_op jit(solution)/shard_map/reduce_scatter | solution.py:52
  404.0 0.0 copy-done.3
  404.0 0.0 copy-done.6
  404.0 1.8 multiply_convert_fusion
  405.8 0.0 all-gather.7.cloned.1.call-update
  405.8 0.6 all-reduce.6.cloned.1.call-start
  406.5 25.2 %all-gather.7.cloned.1.call-done = bf16[512,1792]{1,0:T(8,128)(2,1)} async-done(((bf16[64,1792]{1,0:T(8,128)(2,1)}), bf16[512,1792]{1,0:T(8,128)(2,1)}) %all-gather.7.cloned.1.call-update) | async-done | bytes 1835024 | tf_op jit(solution)/shard_map/all_gather | solution.py:54
  431.6 16.5 %convolution_convert_fusion = bf16[512,2048]{1,0:T(8,128)(2,1)} fusion(bf16[512,1792]{1,0:T(8,128)(2,1)} %all-gather.7.cloned.1.call-done, f32[2048,1792]{1,0:T(8,128)} %param.14), kind=kOutput, calls=%fused_computation.15 | convolution fusion | flops 22549626880 | bytes 18612224 | tf_op jit(solution)/shard_map/dot_general | solution.py:58
  448.2 0.0 all-reduce.6.cloned.1.call-update
  448.2 0.0 all-reduce.8.cloned.1.call-start
  448.3 6.5 %multiply_reduce_fusion = f32[2048]{0:T(1024)S(1)} fusion(f32[2048,1792]{1,0:T(8,128)} %param.14), kind=kLoop, calls=%fused_computation.1 | loop fusion | flops 7337984 | bytes 14688256 | tf_op jit(solution)/shard_map/reduce_sum | solution.py:45
  454.8 0.0 copy-start.2
  454.8 0.1 broadcast_select_fusion
  454.9 16.4 %psum.31 = f32[2,2048]{1,0:T(2,128)S(1)} all-reduce(f32[2,2048]{1,0:T(2,128)S(1)} %broadcast_select_fusion), channel_id=1, replica_groups=mesh['mp'=2,'width'=2,'hidden'=8] {'mp','width'}, use_global_device_ids=true, to_apply=%region_7.8 | all-reduce | flops 4096 | bytes 32768 | tf_op jit(solution)/shard_map/psum | solution.py:47
  471.3 40.0 %all-reduce.6.cloned.1.call-done = bf16[512,2048]{1,0:T(8,128)(2,1)} async-done(((bf16[512,2048]{1,0:T(8,128)(2,1)}), bf16[512,2048]{1,0:T(8,128)(2,1)}) %all-reduce.6.cloned.1.call-update) | async-done | bytes 2097168 | tf_op jit(solution)/shard_map/psum | solution.py:15
  511.3 0.0 all-reduce.8.cloned.1.call-update
  511.3 0.7 convert_bitcast_fusion
  512.0 0.0 copy-done.2
  512.0 0.9 convert_reduce_fusion
  512.9 18.9 %multiply_add_fusion = f32[2048,1792]{1,0:T(8,128)} fusion(f32[2048,1792]{1,0:T(8,128)} %param.14, f32[512,2048]{1,0:T(8,128)} %copy-done, bf16[512,1792]{1,0:T(8,128)(2,1)S(1)} %copy-done.2, f32[2048]{0:T(1024)S(1)} %divide_multiply_fusion.1), kind=kOutput, calls=%fused_computation | convolution fusion | flops 22555918336 | bytes 35397632 | tf_op jit(solution)/shard_map/dot_general | solution.py:71
  531.8 44.8 %all-reduce.8.cloned.1.call-done = bf16[512,2048]{1,0:T(8,128)(2,1)} async-done(((bf16[512,2048]{1,0:T(8,128)(2,1)}), bf16[512,2048]{1,0:T(8,128)(2,1)}) %all-reduce.8.cloned.1.call-update) | async-done | bytes 2097168 | tf_op jit(solution)/shard_map/psum | solution.py:16
  576.6 0.0 copy-start.1
  576.6 0.0 copy-start.4
  576.6 5.0 fusion.22
  581.5 0.0 copy-done.1
  581.6 0.0 copy-done.4
  581.6 17.9 %fusion.23 = f32[1792,2048]{1,0:T(8,128)} fusion(bf16[512,1792]{1,0:T(8,128)(2,1)} %all-gather.5.cloned.1.call-done, bf16[512,2048]{1,0:T(8,128)(2,1)S(1)} %copy-done.4, f32[512,2048]{1,0:T(8,128)S(1)} %copy-done.1, f32[2048]{0:T(1024)S(1)} %bitcast.33, f32[2048]{0:T(1024)S(1)} %copy-done.5), kind=kOutput, calls=%fused_computation.34 | convolution fusion | flops 22556966912 | bytes 22822912 | tf_op jit(solution)/shard_map/dot_general | solution.py:66
  (5 shorter events, 0.1 us)
Async XLA Ops:
  7.2 47.7 %all-gather.9.cloned.1.call-start = ((), (), s32[]{:S(2)}) async-start(), calls=%async_computation.11 | async-start | bytes 4128768 | tf_op jit(solution)/shard_map/all_gather | solution.py:27
  7.9 148.5 %reduce-scatter.4.cloned.1.call-start = ((), (), s32[]{:S(2)}) async-start(), calls=%async_computation.3 | async-start | bytes 8257536 | tf_op jit(solution)/shard_map/reduce_scatter | solution.py:34
  54.9 9.6 %copy-start.7 = (bf16[1,512,3584]{2,1,0:T(8,128)(2,1)S(1)}, bf16[1,512,3584]{2,1,0:T(8,128)(2,1)}, u32[]{:S(2)}) copy-start(bf16[1,512,3584]{2,1,0:T(8,128)(2,1)} %all-gather.9.cloned.1.call-done) | copy-start | bytes 11010052
  54.9 16.8 %slice-start = ((s8[6422528]{0:T(1024)(128)(4,1)}), s8[4194304]{0:T(1024)(128)(4,1)S(1)}, s32[]{:S(2)}) async-start(s8[6422528]{0:T(1024)(128)(4,1)} %bitcast.35), calls=%async_computation.12 | async-start | bytes 8388608
  64.6 7.2 %slice-start.1 = ((s8[6422528]{0:T(1024)(128)(4,1)}), s8[2228224]{0:T(1024)(128)(4,1)S(1)}, s32[]{:S(2)}) async-start(s8[6422528]{0:T(1024)(128)(4,1)} %bitcast.35), calls=%async_computation.13 | async-start | bytes 4456448
  77.8 98.3 %reduce-scatter.6.cloned.1.call-start = ((), (), s32[]{:S(2)}) async-start(), calls=%async_computation.4 | async-start | bytes 1376256 | tf_op jit(solution)/shard_map/reduce_scatter | solution.py:40
  156.4 48.7 %all-gather.5.cloned.1.call-start = ((), (), s32[]{:S(2)}) async-start(), calls=%async_computation.5 | async-start | bytes 2064384 | tf_op jit(solution)/shard_map/all_gather | solution.py:42
  177.9 147.4 %all-reduce.4.cloned.1.call-start = ((), (), s32[]{:S(2)}) async-start(), calls=%async_computation.6 | async-start | bytes 8388608 | tf_op jit(solution)/shard_map/psum | solution.py:47
  222.1 103.2 %copy-start.5 = (f32[2048]{0:T(1024)S(1)}, f32[2048]{0:T(1024)}, u32[]{:S(2)}) copy-start(f32[2048]{0:T(1024)} %param.13) | copy-start | bytes 24580
  222.1 181.9 %reduce-scatter.8.cloned.1.call-start = ((), (), s32[]{:S(2)}) async-start(), calls=%async_computation.7 | async-start | bytes 4128768 | tf_op jit(solution)/shard_map/reduce_scatter | solution.py:52
  330.2 2.0 copy-start
  332.2 71.8 %copy-start.3 = (f32[64,1792]{1,0:T(8,128)S(1)}, f32[64,1792]{1,0:T(8,128)}, u32[]{:S(2)}) copy-start(f32[64,1792]{1,0:T(8,128)} %reduce-scatter.6.cloned.1.call-done) | copy-start | bytes 1376260
  332.2 71.8 %copy-start.6 = (f32[1792]{0:T(1024)S(1)}, f32[1792]{0:T(1024)}, u32[]{:S(2)}) copy-start(f32[1792]{0:T(1024)} %param.15) | copy-start | bytes 21508
  358.9 72.8 %all-gather.7.cloned.1.call-start = ((), (), s32[]{:S(2)}) async-start(), calls=%async_computation.8 | async-start | bytes 2064384 | tf_op jit(solution)/shard_map/all_gather | solution.py:54
  405.8 105.5 %all-reduce.6.cloned.1.call-start = ((), (), s32[]{:S(2)}) async-start(), calls=%async_computation.9 | async-start | bytes 4194304 | tf_op jit(solution)/shard_map/psum | solution.py:15
  448.2 128.4 %all-reduce.8.cloned.1.call-start = ((), (), s32[]{:S(2)}) async-start(), calls=%async_computation.10 | async-start | bytes 4194304 | tf_op jit(solution)/shard_map/psum | solution.py:16
  454.8 57.3 %copy-start.2 = (bf16[512,1792]{1,0:T(8,128)(2,1)S(1)}, bf16[512,1792]{1,0:T(8,128)(2,1)}, u32[]{:S(2)}) copy-start(bf16[512,1792]{1,0:T(8,128)(2,1)} %all-gather.7.cloned.1.call-done) | copy-start | bytes 5505028
  576.6 5.0 copy-start.1
  576.6 5.0 copy-start.4
Sparse Core Ops, SparseCore 0:
  9.6 45.2 all-gather.8
  77.9 78.4 reduce-scatter.3
  158.7 17.3 reduce-scatter.5
  178.2 26.9 all-gather.4
  222.2 103.0 all-reduce.3
  359.0 44.9 reduce-scatter.7
  406.2 25.3 all-gather.6
  448.3 62.8 all-reduce.5
  513.6 62.9 all-reduce.7
